TPU v7x, 32 devices: a whole 2x2x4 slice. The times are simulated.
32 devices in a mesh: dp: 4 (over y, x), filter: 8 (over z, core).
Axes of the slice: x: 2, y: 2, z: 4, core: 2. Of those that a mesh axis runs over, the one named last changes fastest.
Arguments:
- fields: bfloat16 [4, 32, 32, 1024], P('dp', None, None, 'filter'), may hold values from -6 to 6
- weight_one: bfloat16 [3, 3, 1024, 1024], P(None, None, 'dp', 'filter'), may hold values from -0.0625 to 0.0625
- weight_two: bfloat16 [3, 3, 1024, 1024], P(None, None, 'dp', 'filter'), may hold values from -0.0625 to 0.0625
- cotangent: bfloat16 [4, 32, 32, 1024], P('dp', None, None, 'filter'), may hold values from -6 to 6
Outputs:
- output: bfloat16 [4, 32, 32, 1024], P('dp', None, None, 'filter')
- grad_one: float32 [3, 3, 1024, 1024], P(None, None, 'dp', 'filter')
- grad_two: float32 [3, 3, 1024, 1024], P(None, None, 'dp', 'filter')
All inputs are finite; a program needn't handle non-finite values.
Results may differ from a plain program's by a relative error of at most 0.018.
Values may be sent and summed in bfloat16 or wider, within the bound.
No kernel may reach another device: no remote copies, remote signals or barrier semaphores. Data moves between devices by JAX's collectives and lax.ppermute only.
A program may use at most 128 MiB of HBM per device.

v0:
```python
import jax
import jax.numpy as jnp
from jax import lax
from jax.sharding import PartitionSpec as P


def shift_cells(values, row_step, col_step):
    size = values.shape[1]
    padded = jnp.pad(values, ((0, 0), (1, 1), (1, 1), (0, 0)))
    return padded[:, 1 + row_step : 1 + row_step + size, 1 + col_step : 1 + col_step + size, :]


def conv_taps(inputs, weights):
    products = jnp.einsum("bhwc,pqcd->bhwpqd", inputs, weights, preferred_element_type=jnp.float32)
    result = jnp.zeros(inputs.shape[:3] + (weights.shape[3],), jnp.float32)
    for row_tap in range(3):
        for col_tap in range(3):
            result = result + shift_cells(
                products[:, :, :, row_tap, col_tap, :], row_tap - 1, col_tap - 1
            )
    return result


def shifted_stack(grads):
    pieces = []
    for row_tap in range(3):
        for col_tap in range(3):
            pieces.append(shift_cells(grads, 1 - row_tap, 1 - col_tap))
    return jnp.stack(pieces, axis=3).reshape(grads.shape[:3] + (3, 3, grads.shape[3]))


def transposed(grads, weights):
    stacked = shifted_stack(grads)
    return jnp.einsum("bhwpqd,pqcd->bhwc", stacked, weights, preferred_element_type=jnp.float32)


def filter_grads(inputs, grads):
    stacked = shifted_stack(grads)
    return jnp.einsum("bhwc,bhwpqd->pqcd", inputs, stacked, preferred_element_type=jnp.float32)


def body(fields, weight_one, weight_two, cotangent):
    full_one = lax.all_gather(weight_one, "dp", axis=2, tiled=True)
    gathered = lax.all_gather(fields, "filter", axis=3, tiled=True)
    pre_one = conv_taps(gathered, full_one)
    hidden = jax.nn.silu(pre_one).astype(jnp.bfloat16)
    hidden_all = lax.all_gather(hidden, "filter", axis=3, tiled=True)
    full_two = lax.all_gather(weight_two, "dp", axis=2, tiled=True)
    output = conv_taps(hidden_all, full_two).astype(jnp.bfloat16)
    grad_two = lax.psum_scatter(
        filter_grads(hidden_all, cotangent).astype(jnp.bfloat16),
        "dp",
        scatter_dimension=2,
        tiled=True,
    ).astype(jnp.float32)
    partial_back = transposed(cotangent, full_two)
    back = lax.psum_scatter(
        partial_back.astype(jnp.bfloat16), "filter", scatter_dimension=3, tiled=True
    ).astype(jnp.float32)
    sigma = jax.nn.sigmoid(pre_one)
    back_pre = (back * sigma * (1.0 + pre_one * (1.0 - sigma))).astype(jnp.bfloat16)
    grad_one = lax.psum_scatter(
        filter_grads(gathered, back_pre).astype(jnp.bfloat16), "dp", scatter_dimension=2, tiled=True
    ).astype(jnp.float32)
    return (output, grad_one, grad_two)


def solution(mesh):
    placed = (
        P("dp", None, None, "filter"),
        P(None, None, "dp", "filter"),
        P(None, None, "dp", "filter"),
        P("dp", None, None, "filter"),
    )
    return jax.shard_map(
        body,
        mesh=mesh,
        in_specs=placed,
        out_specs=(
            P("dp", None, None, "filter"),
            P(None, None, "dp", "filter"),
            P(None, None, "dp", "filter"),
        ),
        check_vma=False,
    )
```

profile of v0, /device:TPU:0, one launch (start us, length us, event | category | flops | bytes accessed | tf_op | source)
XLA Modules:
  0.0 284.4 jit_solution(1730159838617975054)
XLA Ops:
  7.2 0.7 all-gather.11.cloned.1.call-update
  8.0 0.7 all-gather.7.cloned.1.call-update
  8.7 0.7 all-gather.5.cloned.1.call-update
  9.4 1.0 fusion.41
  10.5 1.0 fusion.43
  12.1 38.0 %all-gather.11.cloned.1.call-done = bf16[3,3,1024,128]{3,2,1,0:T(8,128)(2,1)} async-done(((bf16[3,3,256,128]{3,2,1,0:T(8,128)(2,1)}), bf16[3,3,1024,128]{3,2,1,0:T(8,128)(2,1)}) %all-gather.11.cloned.1.call-update) | async-done | bytes 2359312 | tf_op jit(solution)/shard_map/all_gather | solution.py:48
  50.1 5.3 %fusion.16 = bf16[1,32,32,1024]{3,2,1,0:T(8,128)(2,1)S(1)} fusion(bf16[32,32,3,3,128]{4,1,0,3,2:T(8,128)(2,1)} %bitcast.223, bf16[3,3,1024,128]{3,2,1,0:T(8,128)(2,1)} %all-gather.11.cloned.1.call-done), kind=kOutput, calls=%fused_computation.15 | convolution fusion | flops 2416967680 | bytes 6815744 | tf_op jit(solution)/shard_map/bhwpqd,pqcd->bhwc/dot_general | solution.py:34
  55.4 12.2 %copy.60 = bf16[1,32,32,1024]{2,1,0,3:T(8,128)(2,1)} copy(bf16[1,32,32,1024]{3,2,1,0:T(8,128)(2,1)S(1)} %fusion.16) | data formatting | bytes 4194304
  67.5 12.5 %reshape.42 = bf16[1024,1024]{1,0:T(8,128)(2,1)} reshape(bf16[1024,1,32,32]{3,2,1,0:T(8,128)(2,1)} %bitcast.220) | data formatting | bytes 4194304
  80.0 9.4 %all-gather.7.cloned.1.call-done = bf16[3,3,1024,128]{3,2,1,0:T(8,128)(2,1)} async-done(((bf16[3,3,256,128]{3,2,1,0:T(8,128)(2,1)}), bf16[3,3,1024,128]{3,2,1,0:T(8,128)(2,1)}) %all-gather.7.cloned.1.call-update) | async-done | bytes 2359312 | tf_op jit(solution)/shard_map/all_gather | solution.py:43
  89.4 32.5 %all-gather.5.cloned.1.call-done = bf16[1,32,32,1024]{3,2,1,0:T(8,128)(2,1)} async-done(((bf16[1,32,32,128]{3,2,1,0:T(8,128)(2,1)}), bf16[1,32,32,1024]{3,2,1,0:T(8,128)(2,1)}) %all-gather.5.cloned.1.call-update) | async-done | bytes 2097168 | tf_op jit(solution)/shard_map/all_gather | solution.py:44
  121.9 5.2 %fusion.10 = f32[1,32,32,3,3,128]{5,2,4,3,1,0:T(8,128)S(1)} fusion(bf16[3,3,1024,128]{3,2,1,0:T(8,128)(2,1)} %all-gather.7.cloned.1.call-done, bf16[1,32,32,1024]{3,2,1,0:T(8,128)(2,1)} %all-gather.5.cloned.1.call-done), kind=kOutput, calls=%fused_computation.13 | convolution fusion | flops 2415919104 | bytes 9175040 | tf_op jit(solution)/shard_map/bhwc,pqcd->bhwpqd/dot_general | solution.py:14
  127.1 2.1 copy-done.1
  129.2 1.8 slice_bitcast_fusion.17
  130.9 28.0 %reduce-scatter.10.cloned.1.call-done = bf16[128,1024]{1,0:T(8,128)(2,1)} async-done(((bf16[1024,1024]{1,0:T(8,128)(2,1)}), bf16[128,1024]{1,0:T(8,128)(2,1)}) %reduce-scatter.10.cloned.1.call-update) | async-done | bytes 262160
  158.9 1.8 reshape.43
  160.7 1.8 copy.61
  162.5 2.3 multiply_convert_fusion
  164.8 0.8 multiply_convert_fusion.1
  166.6 0.9 copy-done.5
  167.5 4.0 %fusion = bf16[3,3,1024,128]{2,3,1,0:T(8,128)(2,1)} fusion(bf16[32,32,3,3,128]{4,1,0,3,2:T(8,128)(2,1)S(1)} %bitcast.225, bf16[1,32,32,1024]{3,2,1,0:T(8,128)(2,1)S(1)} %copy-done.5), kind=kOutput, calls=%fused_computation.3 | convolution fusion | flops 2417098752 | bytes 6815744 | tf_op jit(solution)/shard_map/bhwc,bhwpqd->pqcd/dot_general | solution.py:39
  171.6 23.8 %all-gather.9.cloned.1.call-done = bf16[1,32,32,1024]{3,2,1,0:T(8,128)(2,1)} async-done(((bf16[1,32,32,128]{3,2,1,0:T(8,128)(2,1)}), bf16[1,32,32,1024]{3,2,1,0:T(8,128)(2,1)}) %all-gather.9.cloned.1.call-update) | async-done | bytes 2097168 | tf_op jit(solution)/shard_map/all_gather | solution.py:47
  195.4 4.2 %fusion.4 = bf16[3,3,128,1024,1]{3,2,0,1,4:T(8,128)(2,1)S(1)} fusion(bf16[32,32,3,3,128]{4,1,0,3,2:T(8,128)(2,1)S(1)} %bitcast.224, bf16[1,32,32,1024]{3,2,1,0:T(8,128)(2,1)} %all-gather.9.cloned.1.call-done), kind=kOutput, calls=%fused_computation.7 | convolution fusion | flops 2415919104 | bytes 6815744 | tf_op jit(solution)/shard_map/bhwc,bhwpqd->pqcd/dot_general | solution.py:39
  199.6 1.7 copy.83
  201.4 1.6 copy-done.4
  203.0 4.8 %fusion.13 = f32[1,32,32,3,3,128]{5,2,4,3,1,0:T(8,128)S(1)} fusion(bf16[3,3,1024,128]{3,2,1,0:T(8,128)(2,1)S(1)} %copy-done.4, bf16[1,32,32,1024]{3,2,1,0:T(8,128)(2,1)} %all-gather.9.cloned.1.call-done), kind=kOutput, calls=%fused_computation.14 | convolution fusion | flops 2415919104 | bytes 9175040 | tf_op jit(solution)/shard_map/bhwc,pqcd->bhwpqd/dot_general | solution.py:14
  207.8 0.7 slice_bitcast_fusion
  208.5 1.3 fusion.39
  209.8 25.0 %reduce-scatter.6.cloned.1.call-done = bf16[3,3,256,128]{2,3,1,0:T(8,128)(2,1)} async-done(((bf16[3,3,1024,128]{2,3,1,0:T(8,128)(2,1)}), bf16[3,3,256,128]{2,3,1,0:T(8,128)(2,1)}) %reduce-scatter.6.cloned.1.call-update) | async-done | bytes 589840 | tf_op jit(solution)/shard_map/reduce_scatter | solution.py:62
  234.8 2.3 copy.45
  237.1 38.2 %reduce-scatter.8.cloned.1.call-done = bf16[3,3,256,128]{2,3,1,0:T(8,128)(2,1)} async-done(((bf16[3,3,1024,128]{2,3,1,0:T(8,128)(2,1)}), bf16[3,3,256,128]{2,3,1,0:T(8,128)(2,1)}) %reduce-scatter.8.cloned.1.call-update) | async-done | bytes 589840 | tf_op jit(solution)/shard_map/reduce_scatter | solution.py:50
  275.3 2.3 copy.46
  (36 shorter events, 1.8 us)
Async XLA Ops:
  7.2 4.3 %copy-start = (bf16[1,32,32,128]{3,2,1,0:T(8,128)(2,1)S(1)}, bf16[1,32,32,128]{3,2,1,0:T(8,128)(2,1)}, u32[]{:S(2)}) copy-start(bf16[1,32,32,128]{3,2,1,0:T(8,128)(2,1)} %param.7) | copy-start | bytes 786436
  7.2 42.9 %all-gather.11.cloned.1.call-start = ((), (), s32[]{:S(2)}) async-start(), calls=%async_computation.6 | async-start | bytes 2949120 | tf_op jit(solution)/shard_map/all_gather | solution.py:48
  7.9 81.5 %all-gather.7.cloned.1.call-start = ((), (), s32[]{:S(2)}) async-start(), calls=%async_computation.4 | async-start | bytes 2949120 | tf_op jit(solution)/shard_map/all_gather | solution.py:43
  8.7 113.2 %all-gather.5.cloned.1.call-start = ((), (), s32[]{:S(2)}) async-start(), calls=%async_computation.3 | async-start | bytes 2359296 | tf_op jit(solution)/shard_map/all_gather | solution.py:44
  9.4 149.5 %reduce-scatter.10.cloned.1.call-start = ((), (), s32[]{:S(2)}) async-start(), calls=%async_computation.9 | async-start | bytes 2359296
  12.1 38.0 %copy-start.2 = (bf16[1,32,32,9,128]{4,2,1,3,0:T(8,128)(2,1)}, bf16[1,32,32,9,128]{4,2,1,3,0:T(8,128)(2,1)S(1)}, u32[]{:S(2)}) copy-start(bf16[1,32,32,9,128]{4,2,1,3,0:T(8,128)(2,1)S(1)} %fusion.55) | copy-start | bytes 7077892
  80.0 115.4 %all-gather.9.cloned.1.call-start = ((), (), s32[]{:S(2)}) async-start(), calls=%async_computation.5 | async-start | bytes 2359296 | tf_op jit(solution)/shard_map/all_gather | solution.py:47
  127.1 2.1 copy-start.1
  165.7 69.1 %reduce-scatter.6.cloned.1.call-start = ((), (), s32[]{:S(2)}) async-start(), calls=%async_computation.7 | async-start | bytes 2949120 | tf_op jit(solution)/shard_map/reduce_scatter | solution.py:62
  165.9 1.6 copy-start.5
  171.5 23.9 %copy-start.3 = (bf16[1,32,32,9,128]{4,2,1,3,0:T(8,128)(2,1)S(1)}, bf16[1,32,32,9,128]{4,2,1,3,0:T(8,128)(2,1)}, u32[]{:S(2)}) copy-start(bf16[1,32,32,9,128]{4,2,1,3,0:T(8,128)(2,1)} %copy-done.2) | copy-start | bytes 7077892
  171.5 103.8 %reduce-scatter.8.cloned.1.call-start = ((), (), s32[]{:S(2)}) async-start(), calls=%async_computation.8 | async-start | bytes 2949120 | tf_op jit(solution)/shard_map/reduce_scatter | solution.py:50
  201.3 1.7 copy-start.4
Sparse Core Ops, SparseCore 0:
  9.9 40.1 all-gather.10
  51.9 37.4 all-gather.6
  91.0 30.8 all-gather.4
  124.0 34.8 reduce-scatter.9
  165.8 29.5 all-gather.8
  198.3 36.4 reduce-scatter.5
  237.9 37.3 reduce-scatter.7
where the time goes:
time: 285 us; the launch traced here: 284 us
  waiting for transfers between devices  197 us (69%)
  local copies, waits for them, and re-layouts  44.9 us (16%)
  matrix products  23.5 us (8%)
  between operations  14.3 us (5%)
  other arithmetic  4.4 us (2%)
    unnamed x34, local copies, waits for them, and re-layouts  40.6 us
    reduce_scatter x1, waiting for transfers between devices, body(): lax.psum_scatter(filter_grads(hidden_all, cotangent).astype(jnp.bfloat16)...  38.2 us
    all_gather x1, waiting for transfers between devices, body(): full_two = lax.all_gather(weight_two, 'dp', axis=2, tiled=True)  38 us
    all_gather x1, waiting for transfers between devices, body(): gathered = lax.all_gather(fields, 'filter', axis=3, tiled=True)  32.5 us
    unnamed x8, waiting for transfers between devices  30.1 us
    reduce_scatter x1, waiting for transfers between devices, body(): lax.psum_scatter(filter_grads(gathered, back_pre).astype(jnp.bfloat16), '...  25 us
    all_gather x1, waiting for transfers between devices, body(): hidden_all = lax.all_gather(hidden, 'filter', axis=3, tiled=True)  23.8 us
    dot_general x2, matrix products, conv_taps(): jnp.einsum('bhwc,pqcd->bhwpqd', inputs, weights, preferred_element_type=j...  9.99 us
  transfers between devices with their start and end apart: 7, of which 7 were waited for; matrix products, arithmetic and copies ran while one was open for 21% of the time, Pallas kernels for 0%

commit v1 on v0

--- a/solution.py
+++ b/solution.py
@@ -2,6 +2,19 @@
 import jax.numpy as jnp
 from jax import lax
 from jax.sharding import PartitionSpec as P
+from jax.lax import axis_index, axis_size, ppermute
+
+
+def search_face(my_tile, d0):
+    nodes = [my_tile]
+    fan = axis_size("dp")
+    for dd in range(fan - 1):
+        nodes.append(
+            ppermute(nodes[-1], axis_name="dp", perm=[(p, (p + 1) % fan) for p in range(fan)])
+        )
+    return jnp.roll(
+        jnp.concatenate(nodes[::-1], d0), (axis_index("dp") + 1) * my_tile.shape[d0], d0
+    )
 
 
 def shift_cells(values, row_step, col_step):
@@ -45,7 +58,7 @@
     pre_one = conv_taps(gathered, full_one)
     hidden = jax.nn.silu(pre_one).astype(jnp.bfloat16)
     hidden_all = lax.all_gather(hidden, "filter", axis=3, tiled=True)
-    full_two = lax.all_gather(weight_two, "dp", axis=2, tiled=True)
+    full_two = search_face(weight_two, 2)
     output = conv_taps(hidden_all, full_two).astype(jnp.bfloat16)
     grad_two = lax.psum_scatter(
         filter_grads(hidden_all, cotangent).astype(jnp.bfloat16),

time: 285 us -> 265 us (0.930)
  waiting for transfers between devices: 197 us -> 160 us
  local copies, waits for them, and re-layouts: 44.9 us -> 54.6 us
  starting transfers between devices: 0.46 us -> 8.27 us
    ppermute x0 -> x3, waiting for transfers between devices: none -> 44.2 us  [search_face(): ppermute(nodes[-1], axis_name='dp', perm=[(p, (p + 1) % fan) for p in ran...]
    all_gather x1 -> x0, waiting for transfers between devices: 38 us -> none  [body(): full_two = lax.all_gather(weight_two, 'dp', axis=2, tiled=True)]
    all_gather x1, waiting for transfers between devices: 32.5 us -> 0.02 us  [body(): gathered = lax.all_gather(fields, 'filter', axis=3, tiled=True)]
    all_gather x1, waiting for transfers between devices: 9.39 us -> 0.02 us  [body(): full_one = lax.all_gather(weight_one, 'dp', axis=2, tiled=True)]
    unnamed x34 -> x41, local copies, waits for them, and re-layouts: 40.6 us -> 49.5 us
    ppermute x0 -> x3, starting transfers between devices: none -> 7.85 us  [search_face(): ppermute(nodes[-1], axis_name='dp', perm=[(p, (p + 1) % fan) for p in ran...]
    unnamed x8 -> x7, waiting for transfers between devices: 30.1 us -> 28.8 us
  transfers between devices with their start and end apart: 7 -> 9, of which waited for: 7 -> 7; matrix products, arithmetic and copies ran while one was open for 21% -> 25% of each run, Pallas kernels for 0% -> 0%
where the time goes in v1:
time: 265 us
  waiting for transfers between devices  160 us (60%)
  local copies, waits for them, and re-layouts  54.6 us (21%)
  matrix products  23.5 us (9%)
  between operations  14.3 us (5%)
  starting transfers between devices  8.27 us (3%)
  other arithmetic  4.4 us (2%)
    unnamed x41, local copies, waits for them, and re-layouts  49.5 us
    ppermute x3, waiting for transfers between devices, search_face(): ppermute(nodes[-1], axis_name='dp', perm=[(p, (p + 1) % fan) for p in ran...  44.2 us
    reduce_scatter x1, waiting for transfers between devices, body(): lax.psum_scatter(filter_grads(hidden_all, cotangent).astype(jnp.bfloat16)...  38 us
    unnamed x7, waiting for transfers between devices  28.8 us
    reduce_scatter x1, waiting for transfers between devices, body(): lax.psum_scatter(filter_grads(gathered, back_pre).astype(jnp.bfloat16), '...  24.6 us
    all_gather x1, waiting for transfers between devices, body(): hidden_all = lax.all_gather(hidden, 'filter', axis=3, tiled=True)  23.9 us
    dot_general x2, matrix products, conv_taps(): jnp.einsum('bhwc,pqcd->bhwpqd', inputs, weights, preferred_element_type=j...  9.76 us
    dot_general x2, matrix products, filter_grads(): jnp.einsum('bhwc,bhwpqd->pqcd', inputs, stacked, preferred_element_type=j...  8.92 us
  transfers between devices with their start and end apart: 9, of which 7 were waited for; matrix products, arithmetic and copies ran while one was open for 25% of the time, Pallas kernels for 0%

profile of v1, /device:TPU:0, one launch (start us, length us, event | category | flops | bytes accessed | tf_op | source)
XLA Modules:
  0.0 264.6 jit_solution(16128029211350233633)
XLA Ops:
  8.7 3.0 %collective-permute-start = (bf16[3,3,256,128]{3,2,1,0:T(8,128)(2,1)}, bf16[3,3,256,128]{3,2,1,0:T(8,128)(2,1)S(1)}, u32[]{:S(2)}, u32[]{:S(2)}) collective-permute-start(bf16[3,3,256,128]{3,2,1,0:T(8,128)(2,1)} %param.6), channel_id=1, source_target_pairs={{0,8},{8,16},{16,24},{24,0},{1,9},{9,17},{17,25},{25,1},{2,10},{10... | collective-permute-start | bytes 1769480 | tf_op jit(solution)/shard_map/ppermute | solution.py:13
  11.7 18.0 %collective-permute-done = bf16[3,3,256,128]{3,2,1,0:T(8,128)(2,1)S(1)} collective-permute-done((bf16[3,3,256,128]{3,2,1,0:T(8,128)(2,1)}, bf16[3,3,256,128]{3,2,1,0:T(8,128)(2,1)S(1)}, u32[]{:S(2)}, u32[]{:S(2)}) %collective-permute-start) | collective-permute-done | bytes 589856 | tf_op jit(solution)/shard_map/ppermute | solution.py:13
  29.7 2.4 collective-permute-start.1
  32.1 1.7 fusion.43
  33.8 1.6 fusion.45
  35.4 1.7 fusion.47
  37.9 13.2 %collective-permute-done.1 = bf16[3,3,256,128]{3,2,1,0:T(8,128)(2,1)S(1)} collective-permute-done((bf16[3,3,256,128]{3,2,1,0:T(8,128)(2,1)S(1)}, bf16[3,3,256,128]{3,2,1,0:T(8,128)(2,1)S(1)}, u32[]{:S(2)}, u32[]{:S(2)}) %collective-permute-start.1) | collective-permute-done | bytes 589856 | tf_op jit(solution)/shard_map/ppermute | solution.py:13
  51.1 2.5 collective-permute-start.2
  57.4 13.0 %collective-permute-done.2 = bf16[3,3,256,128]{3,2,1,0:T(8,128)(2,1)S(1)} collective-permute-done((bf16[3,3,256,128]{3,2,1,0:T(8,128)(2,1)S(1)}, bf16[3,3,256,128]{3,2,1,0:T(8,128)(2,1)S(1)}, u32[]{:S(2)}, u32[]{:S(2)}) %collective-permute-start.2) | collective-permute-done | bytes 589856 | tf_op jit(solution)/shard_map/ppermute | solution.py:13
  71.1 2.2 copy-done.3
  73.3 4.9 %fusion.16 = bf16[1,32,32,1024]{3,2,1,0:T(8,128)(2,1)S(1)} fusion(bf16[32,32,3,3,128]{4,1,0,3,2:T(8,128)(2,1)} %bitcast.38, bf16[3,3,2048,128]{3,2,1,0:T(8,128)(2,1)S(1)} %constant_dynamic-update-slice_fusion, s32[]{:T(128)S(6)} %select_n.14), kind=kOutput, calls=%fused_computation.15 | convolution fusion | flops 2416967680 | bytes 6815748 | tf_op jit(solution)/shard_map/bhwpqd,pqcd->bhwc/dot_general | solution.py:47
  78.2 12.2 %copy.60 = bf16[1,32,32,1024]{2,1,0,3:T(8,128)(2,1)} copy(bf16[1,32,32,1024]{3,2,1,0:T(8,128)(2,1)S(1)} %fusion.16) | data formatting | bytes 4194304
  90.3 12.4 %reshape.42 = bf16[1024,1024]{1,0:T(8,128)(2,1)} reshape(bf16[1024,1,32,32]{3,2,1,0:T(8,128)(2,1)} %bitcast.220) | data formatting | bytes 4194304
  102.9 5.2 %fusion.10 = f32[1,32,32,3,3,128]{5,2,4,3,1,0:T(8,128)S(1)} fusion(bf16[3,3,1024,128]{3,2,1,0:T(8,128)(2,1)} %all-gather.6.cloned.1.call-done, bf16[1,32,32,1024]{3,2,1,0:T(8,128)(2,1)} %all-gather.4.cloned.1.call-done), kind=kOutput, calls=%fused_computation.13 | convolution fusion | flops 2415919104 | bytes 9175040 | tf_op jit(solution)/shard_map/bhwc,pqcd->bhwpqd/dot_general | solution.py:27
  108.0 2.1 copy-done.1
  110.2 1.8 slice_bitcast_fusion.17
  111.9 27.3 %reduce-scatter.10.cloned.1.call-done = bf16[128,1024]{1,0:T(8,128)(2,1)} async-done(((bf16[1024,1024]{1,0:T(8,128)(2,1)}), bf16[128,1024]{1,0:T(8,128)(2,1)}) %reduce-scatter.10.cloned.1.call-update) | async-done | bytes 262160
  139.2 1.8 reshape.43
  141.1 1.8 copy.61
  142.9 2.3 multiply_convert_fusion
  147.0 0.9 copy-done.4
  147.8 4.0 %fusion = bf16[3,3,1024,128]{2,3,1,0:T(8,128)(2,1)} fusion(bf16[32,32,3,3,128]{4,1,0,3,2:T(8,128)(2,1)S(1)} %bitcast.223, bf16[1,32,32,1024]{3,2,1,0:T(8,128)(2,1)S(1)} %copy-done.4), kind=kOutput, calls=%fused_computation.3 | convolution fusion | flops 2417098752 | bytes 6815744 | tf_op jit(solution)/shard_map/bhwc,bhwpqd->pqcd/dot_general | solution.py:52
  151.9 23.9 %all-gather.8.cloned.1.call-done = bf16[1,32,32,1024]{3,2,1,0:T(8,128)(2,1)} async-done(((bf16[1,32,32,128]{3,2,1,0:T(8,128)(2,1)}), bf16[1,32,32,1024]{3,2,1,0:T(8,128)(2,1)}) %all-gather.8.cloned.1.call-update) | async-done | bytes 2097168 | tf_op jit(solution)/shard_map/all_gather | solution.py:60
  175.8 4.9 %fusion.4 = bf16[3,3,128,1024,1]{3,2,0,1,4:T(8,128)(2,1)S(1)} fusion(bf16[32,32,3,3,128]{4,1,0,3,2:T(8,128)(2,1)} %bitcast.38, bf16[1,32,32,1024]{3,2,1,0:T(8,128)(2,1)} %all-gather.8.cloned.1.call-done), kind=kOutput, calls=%fused_computation.7 | convolution fusion | flops 2415919104 | bytes 6815744 | tf_op jit(solution)/shard_map/bhwc,bhwpqd->pqcd/dot_general | solution.py:52
  180.7 1.7 copy.83
  182.4 1.6 copy-done.5
  184.0 4.6 %fusion.13 = f32[1,32,32,3,3,128]{5,2,4,3,1,0:T(8,128)S(1)} fusion(bf16[1,32,32,1024]{3,2,1,0:T(8,128)(2,1)S(1)} %copy-done.5, bf16[3,3,2048,128]{3,2,1,0:T(8,128)(2,1)} %copy-done.3, s32[]{:T(128)S(6)} %select_n.14), kind=kOutput, calls=%fused_computation.14 | convolution fusion | flops 2415919104 | bytes 9175044 | tf_op jit(solution)/shard_map/bhwc,pqcd->bhwpqd/dot_general | solution.py:27
  189.3 1.3 fusion.41
  190.6 24.6 %reduce-scatter.6.cloned.1.call-done = bf16[3,3,256,128]{2,3,1,0:T(8,128)(2,1)} async-done(((bf16[3,3,1024,128]{2,3,1,0:T(8,128)(2,1)}), bf16[3,3,256,128]{2,3,1,0:T(8,128)(2,1)}) %reduce-scatter.6.cloned.1.call-update) | async-done | bytes 589840 | tf_op jit(solution)/shard_map/reduce_scatter | solution.py:75
  215.1 2.3 copy.45
  217.5 38.0 %reduce-scatter.8.cloned.1.call-done = bf16[3,3,256,128]{2,3,1,0:T(8,128)(2,1)} async-done(((bf16[3,3,1024,128]{2,3,1,0:T(8,128)(2,1)}), bf16[3,3,256,128]{2,3,1,0:T(8,128)(2,1)}) %reduce-scatter.8.cloned.1.call-update) | async-done | bytes 589840 | tf_op jit(solution)/shard_map/reduce_scatter | solution.py:63
  255.5 2.3 copy.46
  (47 shorter events, 9.3 us)
Async XLA Ops:
  7.2 30.0 %copy-start = (bf16[1,32,32,128]{3,2,1,0:T(8,128)(2,1)S(1)}, bf16[1,32,32,128]{3,2,1,0:T(8,128)(2,1)}, u32[]{:S(2)}) copy-start(bf16[1,32,32,128]{3,2,1,0:T(8,128)(2,1)} %param.7) | copy-start | bytes 786436
  7.2 95.7 %all-gather.6.cloned.1.call-start = ((), (), s32[]{:S(2)}) async-start(), calls=%async_computation.4 | async-start | bytes 2949120 | tf_op jit(solution)/shard_map/all_gather | solution.py:56
  7.9 94.9 %all-gather.4.cloned.1.call-start = ((), (), s32[]{:S(2)}) async-start(), calls=%async_computation.3 | async-start | bytes 2359296 | tf_op jit(solution)/shard_map/all_gather | solution.py:57
  8.7 130.6 %reduce-scatter.10.cloned.1.call-start = ((), (), s32[]{:S(2)}) async-start(), calls=%async_computation.8 | async-start | bytes 2359296
  8.7 21.0 %collective-permute-start = (bf16[3,3,256,128]{3,2,1,0:T(8,128)(2,1)}, bf16[3,3,256,128]{3,2,1,0:T(8,128)(2,1)S(1)}, u32[]{:S(2)}, u32[]{:S(2)}) collective-permute-start(bf16[3,3,256,128]{3,2,1,0:T(8,128)(2,1)} %param.6), channel_id=1, source_target_pairs={{0,8},{8,16},{16,24},{24,0},{1,9},{9,17},{17,25},{25,1},{2,10},{10... | collective-permute-start | bytes 1769480 | tf_op jit(solution)/shard_map/ppermute | solution.py:13
  29.7 21.5 %collective-permute-start.1 = (bf16[3,3,256,128]{3,2,1,0:T(8,128)(2,1)S(1)}, bf16[3,3,256,128]{3,2,1,0:T(8,128)(2,1)S(1)}, u32[]{:S(2)}, u32[]{:S(2)}) collective-permute-start(bf16[3,3,256,128]{3,2,1,0:T(8,128)(2,1)S(1)} %collective-permute-done), channel_id=1, source_target_pairs={{0,8},{8,16},{16,24},{24,0},{1,9},{9,17},{17,25},{25,1},{2,10},{10... | collective-permute-start | bytes 1769480 | tf_op jit(solution)/shard_map/ppermute | solution.py:13
  51.1 19.3 %collective-permute-start.2 = (bf16[3,3,256,128]{3,2,1,0:T(8,128)(2,1)S(1)}, bf16[3,3,256,128]{3,2,1,0:T(8,128)(2,1)S(1)}, u32[]{:S(2)}, u32[]{:S(2)}) collective-permute-start(bf16[3,3,256,128]{3,2,1,0:T(8,128)(2,1)S(1)} %collective-permute-done.1), channel_id=1, source_target_pairs={{0,8},{8,16},{16,24},{24,0},{1,9},{9,17},{17,25},{25,1},{2,10},{10... | collective-permute-start | bytes 1769480 | tf_op jit(solution)/shard_map/ppermute | solution.py:13
  55.9 14.8 %copy-start.2 = (bf16[3,3,256,128]{3,2,1,0:T(8,128)(2,1)S(1)}, bf16[3,3,256,128]{3,2,1,0:T(8,128)(2,1)}, u32[]{:S(2)}) copy-start(bf16[3,3,256,128]{3,2,1,0:T(8,128)(2,1)} %param.6) | copy-start | bytes 1769476
  71.1 2.2 copy-start.3
  102.8 73.0 %all-gather.8.cloned.1.call-start = ((), (), s32[]{:S(2)}) async-start(), calls=%async_computation.5 | async-start | bytes 2359296 | tf_op jit(solution)/shard_map/all_gather | solution.py:60
  108.0 2.1 copy-start.1
  146.0 69.1 %reduce-scatter.6.cloned.1.call-start = ((), (), s32[]{:S(2)}) async-start(), calls=%async_computation.6 | async-start | bytes 2949120 | tf_op jit(solution)/shard_map/reduce_scatter | solution.py:75
  146.2 1.6 copy-start.4
  151.8 103.6 %reduce-scatter.8.cloned.1.call-start = ((), (), s32[]{:S(2)}) async-start(), calls=%async_computation.7 | async-start | bytes 2949120 | tf_op jit(solution)/shard_map/reduce_scatter | solution.py:63
  182.4 1.6 copy-start.5
Sparse Core Ops, SparseCore 0:
  9.9 55.4 all-gather.5
  66.9 30.6 all-gather.3
  102.9 36.3 reduce-scatter.9
  146.1 29.5 all-gather.7
  178.7 36.4 reduce-scatter.5
  218.0 37.3 reduce-scatter.7
